TPU v7x, 512 devices: a whole 4x8x8 slice. The times are simulated.
512 devices in a mesh: fsdp: 64 (over z, x, y_lo), tp: 8 (over y_hi, core).
Axes of the slice: x: 4, y: 8 (y_hi: 4, y_lo: 2; y = y_hi * 2 + y_lo), z: 8, core: 2. Of those that a mesh axis runs over, the one named last changes fastest.
Arguments:
- gate_pre: bfloat16 [8192, 14336], P('fsdp', 'tp'), may hold values from -6 to 6
- up_pre: bfloat16 [8192, 14336], P('fsdp', 'tp'), may hold values from -6 to 6
- down_weight: bfloat16 [14336, 4096], P('tp', 'fsdp'), may hold values from -0.046875 to 0.046875
Outputs:
- mixed: bfloat16 [8192, 4096], P('fsdp', 'tp')
All inputs are finite; a program needn't handle non-finite values.
Results may differ from a plain program's by a relative error of at most 0.0049.
Values may be sent and summed in bfloat16 or wider, within the bound.
A program may use at most 64 MiB of HBM per device.

v0:
```python
import jax
import jax.numpy as jnp
from jax import lax
from jax.sharding import PartitionSpec as P


def shards(gate_pre, up_pre, down_weight):
    hidden = (jax.nn.silu(gate_pre.astype(jnp.float32)) * up_pre.astype(jnp.float32)).astype(
        jnp.bfloat16
    )
    terms = jnp.dot(
        hidden,
        lax.all_gather(down_weight, "fsdp", axis=1, tiled=True),
        preferred_element_type=jnp.float32,
    )
    totals = lax.psum(terms, "tp")
    share = totals.shape[1] // lax.axis_size("tp")
    result = lax.dynamic_slice_in_dim(totals, lax.axis_index("tp") * share, share, 1)
    return result.astype(jnp.bfloat16)


def solution(mesh):
    return jax.shard_map(
        shards,
        mesh=mesh,
        in_specs=(P("fsdp", "tp"), P("fsdp", "tp"), P("tp", "fsdp")),
        out_specs=P("fsdp", "tp"),
        check_vma=False,
    )
```

profile of v0, /device:TPU:1, one launch (start us, length us, event | category | flops | bytes accessed | tf_op | source)
XLA Modules:
  0.0 456.0 jit_solution(7326851797001008196)
XLA Ops:
  6.5 0.0 all-gather.2.cloned.1.call-start
  6.5 0.7 all-gather.2.cloned.1.call-update
  7.3 331.1 %all-gather.2.cloned.1.call-done = bf16[1792,4096]{0,1:T(8,128)(2,1)} async-done(((bf16[1792,64]{0,1:T(8,128)(2,1)}), bf16[1792,4096]{0,1:T(8,128)(2,1)}) %all-gather.2.cloned.1.call-update) | async-done | bytes 14680080 | tf_op jit(solution)/shard_map/all_gather | solution.py:13
  338.4 10.2 %fusion.5 = f32[128,4096]{1,0:T(8,128)S(1)} fusion(bf16[1792,4096]{0,1:T(8,128)(2,1)} %all-gather.2.cloned.1.call-done, bf16[128,1792]{1,0:T(8,128)(2,1)} %param.4, bf16[128,1792]{1,0:T(8,128)(2,1)} %param.3), kind=kOutput, calls=%fused_computation.7 | convolution fusion | flops 1880883200 | bytes 17694720 | tf_op jit(solution)/shard_map/dot_general | solution.py:11
  348.7 99.8 %all-reduce.1 = bf16[128,4096]{1,0:T(8,128)(2,1)S(1)} all-reduce(f32[128,4096]{1,0:T(8,128)S(1)} %fusion.5), channel_id=1, replica_groups=mesh['fsdp'=64,'tp'=8] {'tp'}, use_global_device_ids=true, to_apply=%region_0.1 | all-reduce | flops 524288 | bytes 3145728 | tf_op jit(solution)/shard_map/psum | solution.py:16
  448.5 0.7 dynamic-slice_convert_fusion
Async XLA Ops:
  6.5 331.9 %all-gather.2.cloned.1.call-start = ((), (), s32[]{:S(2)}) async-start(), calls=%async_computation | async-start | bytes 14909440 | tf_op jit(solution)/shard_map/all_gather | solution.py:13
Sparse Core Ops, SparseCore 0:
  9.4 328.9 all-gather.1
where the time goes:
time: 456 us
  waiting for transfers between devices  332 us (73%)
  blocking collectives  99.8 us (22%)
  between operations  13.4 us (3%)
  matrix products  10.2 us (2%)
    all_gather x1, waiting for transfers between devices, shards(): lax.all_gather(down_weight, 'fsdp', axis=1, tiled=True)  331 us
    psum x1, blocking collectives, shards(): totals = lax.psum(terms, 'tp')  99.8 us
    dot_general x1, matrix products, shards(): jnp.dot(hidden, lax.all_gather(down_weight, 'fsdp', axis=1, tiled=True),...  10.2 us
  transfers between devices with their start and end apart: 1, of which 1 were waited for; matrix products, arithmetic and copies ran while one was open for 0% of the time, Pallas kernels for 0%

commit v1 on v0

--- a/solution.py
+++ b/solution.py
@@ -2,6 +2,12 @@
 import jax.numpy as jnp
 from jax import lax
 from jax.sharding import PartitionSpec as P
+
+
+def process_series_all(z, axis_key):
+    piece_out = lax.all_gather(z, axis_key)
+    reply = jnp.sum(piece_out, axis=0)
+    return reply
 
 
 def shards(gate_pre, up_pre, down_weight):
@@ -13,7 +19,7 @@
         lax.all_gather(down_weight, "fsdp", axis=1, tiled=True),
         preferred_element_type=jnp.float32,
     )
-    totals = lax.psum(terms, "tp")
+    totals = process_series_all(terms, "tp")
     share = totals.shape[1] // lax.axis_size("tp")
     result = lax.dynamic_slice_in_dim(totals, lax.axis_index("tp") * share, share, 1)
     return result.astype(jnp.bfloat16)

time: 456 us -> 557 us (1.22)
  waiting for transfers between devices: 332 us -> 524 us
  blocking collectives: 99.8 us -> 0 us
  other arithmetic: 0 us -> 7.49 us
    all_gather x0 -> x1, waiting for transfers between devices: none -> 192 us  [process_series_all(): piece_out = lax.all_gather(z, axis_key)]
    psum x1 -> x0, blocking collectives: 99.8 us -> none  [shards(): totals = lax.psum(terms, 'tp')]
    reduce_sum x0 -> x1, other arithmetic: none -> 7.49 us  [process_series_all(): reply = jnp.sum(piece_out, axis=0)]
  transfers between devices with their start and end apart: 1 -> 2, of which waited for: 1 -> 2; matrix products, arithmetic and copies ran while one was open for 0% -> 0% of each run, Pallas kernels for 0% -> 0%
where the time goes in v1:
time: 557 us
  waiting for transfers between devices  524 us (94%)
  between operations  13.4 us (2%)
  matrix products  11.6 us (2%)
  other arithmetic  7.49 us (1%)
    all_gather x1, waiting for transfers between devices, shards(): lax.all_gather(down_weight, 'fsdp', axis=1, tiled=True)  331 us
    all_gather x1, waiting for transfers between devices, process_series_all(): piece_out = lax.all_gather(z, axis_key)  192 us
    dot_general x1, matrix products, shards(): jnp.dot(hidden, lax.all_gather(down_weight, 'fsdp', axis=1, tiled=True),...  11.6 us
  transfers between devices with their start and end apart: 2, of which 2 were waited for; matrix products, arithmetic and copies ran while one was open for 0% of the time, Pallas kernels for 0%

profile of v1, /device:TPU:1, one launch (start us, length us, event | category | flops | bytes accessed | tf_op | source)
XLA Modules:
  0.0 557.0 jit_solution(9738195290681244394)
XLA Ops:
  6.5 0.0 all-gather.4.cloned.1.call-start
  6.5 0.7 all-gather.4.cloned.1.call-update
  7.3 0.0 all-gather.6.cloned.1.call-start
  7.3 331.1 %all-gather.4.cloned.1.call-done = bf16[1792,4096]{0,1:T(8,128)(2,1)} async-done(((bf16[1792,64]{0,1:T(8,128)(2,1)}), bf16[1792,4096]{0,1:T(8,128)(2,1)}) %all-gather.4.cloned.1.call-update) | async-done | bytes 14680080 | tf_op jit(solution)/shard_map/all_gather | solution.py:19
  338.4 11.6 %fusion.5 = f32[128,4096]{1,0:T(8,128)} fusion(bf16[1792,4096]{0,1:T(8,128)(2,1)} %all-gather.4.cloned.1.call-done, bf16[128,1792]{1,0:T(8,128)(2,1)} %param.4, bf16[128,1792]{1,0:T(8,128)(2,1)} %param.3), kind=kOutput, calls=%fused_computation.7 | convolution fusion | flops 1880883200 | bytes 17694720 | tf_op jit(solution)/shard_map/dot_general | solution.py:17
  350.0 0.0 all-gather.6.cloned.1.call-update
  350.0 192.0 %all-gather.6.cloned.1.call-done = f32[1024,4096]{1,0:T(8,128)} async-done(((f32[128,4096]{1,0:T(8,128)}), f32[1024,4096]{1,0:T(8,128)}) %all-gather.6.cloned.1.call-update) | async-done | bytes 16777232 | tf_op jit(solution)/shard_map/all_gather | solution.py:8
  542.0 7.5 %reduce_sum.9 = bf16[128,4096]{1,0:T(8,128)(2,1)S(1)} reduce(f32[8,128,4096]{2,1,0:T(8,128)} %bitcast.2, f32[]{:T(128)} %constant.2.clone.1), dimensions={0}, to_apply=%region_0.1 | reduce | flops 3670016 | bytes 17825796 | tf_op jit(solution)/shard_map/reduce_sum | solution.py:9
  549.5 0.7 dynamic-slice_convert_fusion
Async XLA Ops:
  6.5 331.9 %all-gather.4.cloned.1.call-start = ((), (), s32[]{:S(2)}) async-start(), calls=%async_computation | async-start | bytes 14909440 | tf_op jit(solution)/shard_map/all_gather | solution.py:19
  7.3 534.8 %all-gather.6.cloned.1.call-start = ((), (), s32[]{:S(2)}) async-start(), calls=%async_computation.1 | async-start | bytes 18874368 | tf_op jit(solution)/shard_map/all_gather | solution.py:8
Sparse Core Ops, SparseCore 0:
  9.4 328.9 all-gather.3
  350.2 191.8 all-gather.5
